TPU v7x, 32 devices: a whole 2x2x4 slice. The times are simulated.
32 devices in a mesh: grp: 2 (over x), seq: 8 (over z, y), head: 2 (over core).
Axes of the slice: x: 2, y: 2, z: 4, core: 2. Of those that a mesh axis runs over, the one named last changes fastest.
Arguments:
- q_nope: bfloat16 [8, 128, 128], P('grp', ('seq', 'head')), parts along dimension 0, may hold values from -6 to 6
- q_rope: bfloat16 [8, 128, 64], P('grp', ('seq', 'head')), parts along dimension 0, may hold values from -150 to 150
- w_uk: bfloat16 [128, 128, 512], P(('seq', 'head')), may hold values from -0.5 to 0.5
- w_uv: bfloat16 [128, 512, 128], P(('seq', 'head')), may hold values from -1 to 1
- cache: bfloat16 [8, 4096, 576], P('grp', 'seq'), parts along dimension 0, may hold values from -12 to 12
- lengths: int32 [8], P('grp'), parts along dimension 0, may hold values from 2048 to 4096, as said below
- selected: int32 [8, 8, 32], P('grp'), parts along dimension 0, may hold values from 0 to 63, as said below
Outputs:
- attended: bfloat16 [8, 128, 128], P('grp', ('seq', 'head')), parts along dimension 0
- bounds: float32 [8, 8, 64], P('grp', None, 'seq'), parts along dimension 0
There are 2 independent parts, one for each index of `grp`. A program takes and returns all parts, laid end to end along the dimension named above; an argument that names none is the same for every part. Nothing has to cross between parts.
Inputs may be any that keep to these rules, and one draw needn't show every extreme that they name: `lengths`: some request has exactly 4096 cached tokens; every request has 2048 or more. `selected`: for each request and head group the 32 page numbers are distinct and below ceil(lengths[r] / 64); page 0 and the page of the request's last cached token are always among them.
All inputs are finite; a program needn't handle non-finite values.
Results may differ from a plain program's by a relative error of at most 0.0065.
Values may be sent and summed in bfloat16 or wider, within the bound.
A program may use at most 64 MiB of HBM per device.

v0:
```python
import jax
import jax.numpy as jnp
from jax import lax
from jax.sharding import PartitionSpec as P

GH = 16
PAGE = 64


def local(q_nope, q_rope, w_uk, w_uv, cache, lengths, selected):
    seq_count = lax.axis_size("seq")
    head_count = lax.axis_size("head")
    seq_rank = lax.axis_index("seq")
    head_rank = lax.axis_index("head")
    requests = q_nope.shape[0]
    head_block = q_nope.shape[1]
    latent_width = w_uk.shape[2]
    cache_width = cache.shape[2]
    tokens_here = cache.shape[1]
    pages_here = tokens_here // PAGE
    groups = selected.shape[1]
    softmax_scale = (q_nope.shape[2] + q_rope.shape[2]) ** (-0.5)
    query_latent = jnp.einsum(
        "rhn,hnl->rhl", q_nope, w_uk, preferred_element_type=jnp.float32
    ).astype(jnp.bfloat16)
    absorbed = jnp.concatenate([query_latent, q_rope], axis=2)
    queries = lax.all_gather(absorbed, "seq", axis=1, tiled=True)
    heads_here = head_block * seq_count
    position = jnp.arange(heads_here, dtype=jnp.int32)
    global_head = (
        position // head_block * head_count + head_rank
    ) * head_block + position % head_block
    group_of = global_head // GH
    group_hot = group_of[:, None] == jnp.arange(groups, dtype=jnp.int32)[None, :]
    page_number = seq_rank * pages_here + jnp.arange(pages_here, dtype=jnp.int32)
    token_index = seq_rank * tokens_here + jnp.arange(tokens_here, dtype=jnp.int32).reshape(
        pages_here, PAGE
    )
    live_token = token_index[None] < lengths[:, None, None]
    live_page = live_token[:, :, 0]
    page_blocks = cache.reshape(requests, pages_here, PAGE, cache_width)
    page_low = jnp.min(jnp.where(live_token[..., None], page_blocks, jnp.inf), axis=2).astype(
        jnp.float32
    )
    page_high = jnp.max(jnp.where(live_token[..., None], page_blocks, -jnp.inf), axis=2).astype(
        jnp.float32
    )
    page_low = jnp.where(live_page[..., None], page_low, 0.0)
    page_high = jnp.where(live_page[..., None], page_high, 0.0)
    middle = (page_low + page_high) * 0.5
    spread = (page_high - page_low) * 0.5
    query_float = queries.astype(jnp.float32)
    head_bound = softmax_scale * (
        jnp.einsum("rhd,rpd->rhp", query_float, middle, precision=lax.Precision.HIGHEST)
        + jnp.einsum("rhd,rpd->rhp", jnp.abs(query_float), spread, precision=lax.Precision.HIGHEST)
    )
    group_bound = jnp.max(
        jnp.where(group_hot.T[None, :, :, None], head_bound[:, None, :, :], -1e30), axis=2
    )
    group_bound = lax.pmax(group_bound, "head")
    bounds = jnp.where(live_page[:, None, :], group_bound, 0.0)
    picked = jnp.any(selected[:, :, :, None] == page_number[None, None, None, :], axis=2)
    head_pick = jnp.any(group_hot[None, :, :, None] & picked[:, None, :, :], axis=2)
    scores = (
        jnp.einsum("rhd,rtd->rht", queries, cache, preferred_element_type=jnp.float32)
        * softmax_scale
    )
    scores = scores.reshape(requests, heads_here, pages_here, PAGE)
    scores = jnp.where(live_token[:, None], scores, -1e30)
    page_top = jnp.max(scores, axis=3)
    weights = jnp.where(live_token[:, None], jnp.exp(scores - page_top[..., None]), 0.0).astype(
        jnp.bfloat16
    )
    page_total = jnp.sum(weights.astype(jnp.float32), axis=3)
    page_weighted = jnp.einsum(
        "rhpt,rptl->rhpl",
        weights,
        page_blocks[..., :latent_width],
        preferred_element_type=jnp.float32,
    )
    summit = jnp.max(jnp.where(head_pick, page_top, -1e30), axis=2)
    factor = jnp.where(head_pick, jnp.exp(page_top - summit[..., None]), 0.0)
    total = jnp.sum(factor * page_total, axis=2)
    weighted = jnp.einsum("rhp,rhpl->rhl", factor, page_weighted, precision=lax.Precision.HIGHEST)
    gotten = (
        lax.all_to_all(
            summit.reshape(requests, seq_count, head_block),
            "seq",
            split_axis=1,
            concat_axis=1,
            tiled=True,
        ),
        lax.all_to_all(
            total.reshape(requests, seq_count, head_block),
            "seq",
            split_axis=1,
            concat_axis=1,
            tiled=True,
        ),
        lax.all_to_all(
            weighted.reshape(requests, seq_count, head_block, latent_width),
            "seq",
            split_axis=1,
            concat_axis=1,
            tiled=True,
        ),
    )
    highest = jnp.max(gotten[0], axis=1)
    rescale = jnp.exp(gotten[0] - highest[:, None, :])
    own_total = jnp.sum(rescale * gotten[1], axis=1)
    own_weighted = jnp.sum(rescale[..., None] * gotten[2], axis=1)
    latent_out = (own_weighted / own_total[..., None]).astype(jnp.bfloat16)
    attended = jnp.einsum(
        "rhl,hlv->rhv", latent_out, w_uv, preferred_element_type=jnp.float32
    ).astype(jnp.bfloat16)
    return (attended, bounds)


def solution(mesh):
    placed = (
        P("grp", ("seq", "head"), None),
        P("grp", ("seq", "head"), None),
        P(("seq", "head"), None, None),
        P(("seq", "head"), None, None),
        P("grp", "seq", None),
        P("grp"),
        P("grp", None, None),
    )
    return jax.shard_map(
        local,
        mesh=mesh,
        in_specs=placed,
        out_specs=(P("grp", ("seq", "head"), None), P("grp", None, "seq")),
        check_vma=False,
    )
```

profile of v0, /device:TPU:0, one launch (start us, length us, event | category | flops | bytes accessed | tf_op | source)
XLA Modules:
  0.0 88.1 jit_solution(16813406923026156517)
XLA Ops:
  0.7 0.8 copy.102
  1.5 0.4 copy-done
  1.9 0.9 %fusion.3 = bf16[4,8,512]{2,0,1:T(4,128)(2,1)S(1)} fusion(bf16[8,128,512]{2,1,0:T(8,128)(2,1)S(1)} %copy-done, bf16[4,8,128]{2,1,0:T(8,128)(2,1)} %param.7), kind=kOutput, calls=%fused_computation.8 | convolution fusion | flops 4210688 | bytes 1089536 | tf_op jit(solution)/shard_map/rhn,hnl->rhl/dot_general | solution.py:23
  2.9 32.7 %all_gather.3 = bf16[4,64,576]{2,0,1:T(4,128)(2,1)S(1)} all-gather(bf16[4,8,576]{2,0,1:T(4,128)(2,1)S(1)} %pad_maximum_fusion), channel_id=1, replica_groups=mesh['grp'=2,'seq'=8,'head'=2] {'seq'}, dimensions={1}, use_global_device_ids=true | all-gather | bytes 331776 | tf_op jit(solution)/shard_map/all_gather | solution.py:27
  35.5 2.2 %convolution_multiply_fusion = f32[4,64,512]{2,1,0:T(8,128)S(1)} fusion(bf16[4,512,576]{1,2,0:T(8,128)(2,1)} %param.11, bf16[4,64,576]{2,0,1:T(4,128)(2,1)S(1)} %all_gather.3), kind=kOutput, calls=%fused_computation.6 | convolution fusion | flops 151126016 | bytes 3178496 | tf_op jit(solution)/shard_map/rhd,rtd->rht/dot_general | solution.py:65
  37.7 0.2 reshape.136
  38.0 0.7 compare_reduce_fusion
  38.6 0.1 and_reduce_fusion
  38.9 0.4 fusion.6
  39.3 0.6 copy.105
  39.9 5.6 %all-to-all-start = ((f32[4,8,8]{2,0,1:T(4,128)}), f32[4,8,8]{2,0,1:T(4,128)S(1)}, u32[]{:S(2)}, u32[]{:S(2)}) async-start(f32[4,8,8]{2,0,1:T(4,128)} %copy.105), calls=%async_computation | async-start | bytes 32768 | tf_op jit(solution)/shard_map/all_to_all | solution.py:86
  45.5 0.7 convert_reduce_fusion
  46.2 4.3 %copy.106 = bf16[4,512,576]{2,1,0:T(8,128)(2,1)} copy(bf16[4,512,576]{1,2,0:T(8,128)(2,1)} %param.11) | data formatting | bytes 4718592 | tf_op args[4]
  50.6 0.1 copy.114
  50.7 2.7 %select_reduce_fusion.1 = (bf16[4,8,576]{2,1,0:T(8,128)(2,1)S(1)}, bf16[4,8,576]{2,1,0:T(8,128)(2,1)S(1)}) fusion(pred[4,8,64]{2,1,0:T(8,128)(4,1)S(1)} %broadcast_compare_fusion, bf16[4,512,576]{2,1,0:T(8,128)(2,1)} %copy.106), kind=kLoop, calls=%fused_computation.3 | loop fusion | flops 4681728 | bytes 2435072 | tf_op jit(solution)/shard_map/reduce_min | solution.py:42
  53.4 1.0 %convolution_bitcast_fusion = f32[4,64,8,512]{3,1,2,0:T(8,128)S(1)} fusion(bf16[4,8,64,576]{3,2,1,0:T(8,128)(2,1)S(1)} %bitcast.20, f32[4,64,8,64]{3,2,1,0:T(8,128)S(1)} %reshape.136, f32[4,64,8]{1,2,0:T(8,128)S(1)} %fusion.6, pred[4,8,64]{2,1,0:T(8,128)(4,1)S(1)} %broadcast_compare_fusion), kind=kOutput, calls=%fused_computation.4 | convolution fusion | flops 134742016 | bytes 7360512 | tf_op jit(solution)/shard_map/rhpt,rptl->rhpl/dot_general | solution.py:75
  54.4 5.4 %fusion = f32[4,64,1,512]{3,2,1,0:T(1,128)S(1)} fusion(f32[4,64,8,1]{2,3,1,0:T(1,128)S(1)} %copy.114, f32[4,64,8,512]{3,1,2,0:T(8,128)S(1)} %convolution_bitcast_fusion), kind=kOutput, calls=%fused_computation | convolution fusion | flops 12582912 | bytes 4726784 | tf_op jit(solution)/shard_map/rhp,rhpl->rhl/dot_general | solution.py:84
  59.8 0.1 slice_reduce_fusion
  60.0 0.6 copy.108
  60.7 6.0 %all-to-all-start.2 = ((f32[4,8,8]{2,0,1:T(4,128)}), f32[4,8,8]{2,0,1:T(4,128)S(1)}, u32[]{:S(2)}, u32[]{:S(2)}) async-start(f32[4,8,8]{2,0,1:T(4,128)} %copy.108), calls=%async_computation.2 | async-start | bytes 32768 | tf_op jit(solution)/shard_map/all_to_all | solution.py:93
  66.7 0.5 fusion.10
  67.2 0.8 copy.107
  68.0 5.3 %all-to-all-done.2 = f32[4,8,8]{2,0,1:T(4,128)S(1)} async-done(((f32[4,8,8]{2,0,1:T(4,128)}), f32[4,8,8]{2,0,1:T(4,128)S(1)}, u32[]{:S(2)}, u32[]{:S(2)}) %all-to-all-start.2) | async-done | bytes 1056 | tf_op jit(solution)/shard_map/all_to_all | solution.py:93
  73.3 3.5 %all-to-all-start.1 = ((f32[4,8,8,512]{3,2,0,1:T(8,128)}), f32[4,8,8,512]{3,2,0,1:T(8,128)S(1)}, u32[]{:S(2)}, u32[]{:S(2)}) async-start(f32[4,8,8,512]{3,2,0,1:T(8,128)} %copy.107), calls=%async_computation.1 | async-start | bytes 1048576 | tf_op jit(solution)/shard_map/all_to_all | solution.py:100
  76.8 0.8 fusion.4
  77.6 0.1 select_reduce_fusion.2
  77.7 3.4 %pmax.7 = f32[4,8,8]{2,1,0:T(8,128)S(1)} all-reduce(f32[4,8,8]{2,1,0:T(8,128)S(1)} %select_reduce_fusion.2), channel_id=1, replica_groups=mesh['grp'=2,'seq'=8,'head'=2] {'head'}, use_global_device_ids=true, to_apply=%region_12.13 | all-reduce | flops 256 | bytes 2048 | tf_op jit(solution)/shard_map/pmax | solution.py:60
  81.1 0.6 broadcast_select_fusion
  81.8 5.2 %all-to-all-done.1 = f32[4,8,8,512]{3,2,0,1:T(8,128)S(1)} async-done(((f32[4,8,8,512]{3,2,0,1:T(8,128)}), f32[4,8,8,512]{3,2,0,1:T(8,128)S(1)}, u32[]{:S(2)}, u32[]{:S(2)}) %all-to-all-start.1) | async-done | bytes 524320 | tf_op jit(solution)/shard_map/all_to_all | solution.py:100
  87.0 0.1 multiply_reduce_fusion
  87.2 0.2 fusion.5
  87.4 0.6 copy.113
  (25 shorter events, 0.5 us)
Async XLA Ops:
  0.6 1.2 %copy-start = (bf16[8,128,512]{2,1,0:T(8,128)(2,1)S(1)}, bf16[8,128,512]{2,1,0:T(8,128)(2,1)}, u32[]{:S(2)}) copy-start(bf16[8,128,512]{2,1,0:T(8,128)(2,1)} %param.9) | copy-start | bytes 3145732
  2.8 35.1 %copy-start.3 = (s32[4,8,32]{2,1,0:T(8,128)S(1)}, s32[4,8,32]{2,1,0:T(8,128)}, u32[]{:S(2)}) copy-start(s32[4,8,32]{2,1,0:T(8,128)} %param.13) | copy-start | bytes 12292
  2.8 36.0 %copy-start.4 = (s32[4]{0:T(128)S(1)}, s32[4]{0:T(128)}, u32[]{:S(2)}) copy-start(s32[4]{0:T(128)} %param.12) | copy-start | bytes 52
  39.9 20.7 %all-to-all-start = ((f32[4,8,8]{2,0,1:T(4,128)}), f32[4,8,8]{2,0,1:T(4,128)S(1)}, u32[]{:S(2)}, u32[]{:S(2)}) async-start(f32[4,8,8]{2,0,1:T(4,128)} %copy.105), calls=%async_computation | async-start | bytes 32768 | tf_op jit(solution)/shard_map/all_to_all | solution.py:86
  50.7 2.7 %copy-start.1 = (bf16[4,512,576]{2,1,0:T(8,128)(2,1)S(1)}, bf16[4,512,576]{2,1,0:T(8,128)(2,1)}, u32[]{:S(2)}) copy-start(bf16[4,512,576]{2,1,0:T(8,128)(2,1)} %copy.106) | copy-start | bytes 7077892
  60.7 12.6 %all-to-all-start.2 = ((f32[4,8,8]{2,0,1:T(4,128)}), f32[4,8,8]{2,0,1:T(4,128)S(1)}, u32[]{:S(2)}, u32[]{:S(2)}) async-start(f32[4,8,8]{2,0,1:T(4,128)} %copy.108), calls=%async_computation.2 | async-start | bytes 32768 | tf_op jit(solution)/shard_map/all_to_all | solution.py:93
  66.7 20.5 %copy-start.2 = (bf16[8,512,128]{2,1,0:T(8,128)(2,1)S(1)}, bf16[8,512,128]{2,1,0:T(8,128)(2,1)}, u32[]{:S(2)}) copy-start(bf16[8,512,128]{2,1,0:T(8,128)(2,1)} %param.10) | copy-start | bytes 3145732
  73.3 13.7 %all-to-all-start.1 = ((f32[4,8,8,512]{3,2,0,1:T(8,128)}), f32[4,8,8,512]{3,2,0,1:T(8,128)S(1)}, u32[]{:S(2)}, u32[]{:S(2)}) async-start(f32[4,8,8,512]{3,2,0,1:T(8,128)} %copy.107), calls=%async_computation.1 | async-start | bytes 1048576 | tf_op jit(solution)/shard_map/all_to_all | solution.py:100
where the time goes:
time: 88.6 us; the launch traced here: 88.1 us
  blocking collectives  36 us (41%)
  starting transfers between devices  15.1 us (17%)
  matrix products  11 us (12%)
  waiting for transfers between devices  10.5 us (12%)
  local copies, waits for them, and re-layouts  8.85 us (10%)
  other arithmetic  5.68 us (6%)
    all_gather x1, blocking collectives, local(): queries = lax.all_gather(absorbed, 'seq', axis=1, tiled=True)  32.7 us
    unnamed x13, local copies, waits for them, and re-layouts  6.15 us
    all_to_all x1, starting transfers between devices, local(): lax.all_to_all(total.reshape(requests, seq_count, head_block), 'seq', spl...  6.01 us
    all_to_all x1, starting transfers between devices, local(): lax.all_to_all(summit.reshape(requests, seq_count, head_block), 'seq', sp...  5.61 us
    dot_general x1, matrix products, local(): jnp.einsum('rhp,rhpl->rhl', factor, page_weighted, precision=lax.Precisio...  5.37 us
    all_to_all x1, waiting for transfers between devices, local(): lax.all_to_all(total.reshape(requests, seq_count, head_block), 'seq', spl...  5.28 us
    all_to_all x1, waiting for transfers between devices, local(): lax.all_to_all(weighted.reshape(requests, seq_count, head_block, latent_w...  5.23 us
    all_to_all x1, starting transfers between devices, local(): lax.all_to_all(weighted.reshape(requests, seq_count, head_block, latent_w...  3.49 us
  transfers between devices with their start and end apart: 3, of which 2 were waited for; matrix products, arithmetic and copies ran while one was open for 20% of the time, Pallas kernels for 0%

commit v1 on v0

--- a/solution.py
+++ b/solution.py
@@ -24,7 +24,16 @@
         "rhn,hnl->rhl", q_nope, w_uk, preferred_element_type=jnp.float32
     ).astype(jnp.bfloat16)
     absorbed = jnp.concatenate([query_latent, q_rope], axis=2)
-    queries = lax.all_gather(absorbed, "seq", axis=1, tiled=True)
+    ways = lax.axis_size("seq")
+    up = [(d, (d + 1) % ways) for d in range(ways)]
+    down = [(d, (d - 1) % ways) for d in range(ways)]
+    earlier, later = ([absorbed], [absorbed])
+    for _ in range(ways // 2):
+        earlier.append(lax.ppermute(earlier[-1], "seq", up))
+    for _ in range((ways - 1) // 2):
+        later.append(lax.ppermute(later[-1], "seq", down))
+    line = jnp.concatenate([*earlier[::-1], *later[1:]], axis=1)
+    queries = jnp.roll(line, (lax.axis_index("seq") - ways // 2) * absorbed.shape[1], axis=1)
     heads_here = head_block * seq_count
     position = jnp.arange(heads_here, dtype=jnp.int32)
     global_head = (

time: 88.6 us -> 94.2 us (1.063)
  blocking collectives: 36 us -> 3.36 us
  starting transfers between devices: 15.1 us -> 30 us
  local copies, waits for them, and re-layouts: 8.85 us -> 17.2 us
  matrix products: 11 us -> 16.3 us
  waiting for transfers between devices: 10.5 us -> 15.3 us
  other arithmetic: 5.68 us -> 10.1 us
    all_gather x1 -> x0, blocking collectives: 32.7 us -> none  [local(): queries = lax.all_gather(absorbed, 'seq', axis=1, tiled=True)]
    ppermute x0 -> x7, starting transfers between devices: none -> 15.9 us  [the longest x3 12.9 us: local(): later.append(lax.ppermute(later[-1], 'seq', down))]
    ppermute x0 -> x7, waiting for transfers between devices: none -> 8.94 us  [the longest x4 8.65 us: local(): earlier.append(lax.ppermute(earlier[-1], 'seq', up))]
    unnamed x13 -> x37, local copies, waits for them, and re-layouts: 6.15 us -> 13.4 us
    all_to_all x1, waiting for transfers between devices: 5.28 us -> 1.52 us  [local(): lax.all_to_all(total.reshape(requests, seq_count, head_block), 'seq', spl...]
    dot_general x1, matrix products: 1.03 us -> 4.28 us  [local(): jnp.einsum('rhpt,rptl->rhpl', weights, page_blocks[..., :latent_width], p...]
    dot_general x1, matrix products: 5.37 us -> 8.21 us  [local(): jnp.einsum('rhp,rhpl->rhl', factor, page_weighted, precision=lax.Precisio...]
    all_to_all x1, starting transfers between devices: 3.49 us -> 6 us  [local(): lax.all_to_all(weighted.reshape(requests, seq_count, head_block, latent_w...]
  transfers between devices with their start and end apart: 3 -> 10, of which waited for: 2 -> 6; matrix products, arithmetic and copies ran while one was open for 20% -> 33% of each run, Pallas kernels for 0% -> 0%
where the time goes in v1:
time: 94.2 us; the launch traced here: 93.1 us
  starting transfers between devices  30 us (32%)
  local copies, waits for them, and re-layouts  17.2 us (18%)
  matrix products  16.3 us (17%)
  waiting for transfers between devices  15.3 us (16%)
  other arithmetic  10.1 us (11%)
  blocking collectives  3.36 us (4%)
    unnamed x37, local copies, waits for them, and re-layouts  13.4 us
    ppermute x3, starting transfers between devices, local(): later.append(lax.ppermute(later[-1], 'seq', down))  12.9 us
    ppermute x4, waiting for transfers between devices, local(): earlier.append(lax.ppermute(earlier[-1], 'seq', up))  8.65 us
    dot_general x1, matrix products, local(): jnp.einsum('rhp,rhpl->rhl', factor, page_weighted, precision=lax.Precisio...  8.21 us
    all_to_all x1, starting transfers between devices, local(): lax.all_to_all(weighted.reshape(requests, seq_count, head_block, latent_w...  6 us
    all_to_all x1, waiting for transfers between devices, local(): lax.all_to_all(weighted.reshape(requests, seq_count, head_block, latent_w...  4.83 us
    all_to_all x1, starting transfers between devices, local(): lax.all_to_all(summit.reshape(requests, seq_count, head_block), 'seq', sp...  4.5 us
    dot_general x1, matrix products, local(): jnp.einsum('rhpt,rptl->rhpl', weights, page_blocks[..., :latent_width], p...  4.28 us
  transfers between devices with their start and end apart: 10, of which 6 were waited for; matrix products, arithmetic and copies ran while one was open for 33% of the time, Pallas kernels for 0%

profile of v1, /device:TPU:0, one launch (start us, length us, event | category | flops | bytes accessed | tf_op | source)
XLA Modules:
  0.0 93.1 jit_solution(16636368182199368681)
XLA Ops:
  0.6 1.2 %copy-done = bf16[8,128,512]{2,1,0:T(8,128)(2,1)S(1)} copy-done((bf16[8,128,512]{2,1,0:T(8,128)(2,1)S(1)}, bf16[8,128,512]{2,1,0:T(8,128)(2,1)}, u32[]{:S(2)}) %copy-start) | copy-done | bytes 1048600
  1.9 0.9 %fusion.25 = bf16[8,512,4]{1,2,0:T(4,128)(2,1)S(1)} fusion(bf16[8,128,512]{2,1,0:T(8,128)(2,1)S(1)} %copy-done, bf16[4,8,128]{2,1,0:T(8,128)(2,1)} %param.7), kind=kOutput, calls=%fused_computation.66 | convolution fusion | flops 4194304 | bytes 1089536 | tf_op jit(solution)/shard_map/rhn,hnl->rhl/dot_general | solution.py:23
  2.8 1.3 %pad_maximum_fusion = bf16[4,8,576]{2,1,0:T(8,128)(2,1)} fusion(bf16[4,8,64]{2,1,0:T(8,128)(2,1)} %param.8, bf16[4,8,512]{2,1,0:T(8,128)(2,1)S(1)} %bitcast.23), kind=kLoop, calls=%fused_computation.34 | loop fusion | flops 73728 | bytes 73728 | tf_op jit(solution)/shard_map/concatenate | solution.py:26
  4.1 3.0 %collective-permute-start = (bf16[4,8,576]{2,1,0:T(8,128)(2,1)}, bf16[4,8,576]{2,1,0:T(8,128)(2,1)S(1)}, u32[]{:S(2)}, u32[]{:S(2)}) collective-permute-start(bf16[4,8,576]{2,1,0:T(8,128)(2,1)} %pad_maximum_fusion), channel_id=1, source_target_pairs={{0,2},{2,4},{4,6},{6,8},{8,10},{10,12},{12,14},{14,0},{1,3},{3,5},... | collective-permute-start | bytes 110600 | tf_op jit(solution)/shard_map/ppermute | solution.py:32
  7.1 3.0 %collective-permute-start.4 = (bf16[4,8,576]{2,1,0:T(8,128)(2,1)}, bf16[4,8,576]{2,1,0:T(8,128)(2,1)S(1)}, u32[]{:S(2)}, u32[]{:S(2)}) collective-permute-start(bf16[4,8,576]{2,1,0:T(8,128)(2,1)} %pad_maximum_fusion), channel_id=1, source_target_pairs={{0,14},{2,0},{4,2},{6,4},{8,6},{10,8},{12,10},{14,12},{1,15},{3,1}... | collective-permute-start | bytes 110600 | tf_op jit(solution)/shard_map/ppermute | solution.py:34
  11.4 4.4 %copy.102 = bf16[4,512,576]{2,1,0:T(8,128)(2,1)} copy(bf16[4,512,576]{1,2,0:T(8,128)(2,1)} %param.11) | data formatting | bytes 4718592 | tf_op args[4]
  15.7 0.9 broadcast_compare_fusion
  16.6 3.1 %select_reduce_fusion.1 = (bf16[4,8,576]{2,1,0:T(8,128)(2,1)}, bf16[4,8,576]{2,1,0:T(8,128)(2,1)}) fusion(pred[4,8,64]{2,1,0:T(8,128)(4,1)S(1)} %broadcast_compare_fusion, bf16[4,512,576]{2,1,0:T(8,128)(2,1)} %copy.102), kind=kLoop, calls=%fused_computation.3 | loop fusion | flops 4681728 | bytes 2435072 | tf_op jit(solution)/shard_map/reduce_min | solution.py:51
  20.5 6.0 %collective-permute-done.1 = bf16[4,8,576]{2,1,0:T(8,128)(2,1)S(1)} collective-permute-done((bf16[4,8,576]{2,1,0:T(8,128)(2,1)S(1)}, bf16[4,8,576]{2,1,0:T(8,128)(2,1)S(1)}, u32[]{:S(2)}, u32[]{:S(2)}) %collective-permute-start.1) | collective-permute-done | bytes 36896 | tf_op jit(solution)/shard_map/ppermute | solution.py:32
  26.5 0.8 and_reduce_fusion
  27.3 4.8 %collective-permute-start.5 = (bf16[4,8,576]{2,1,0:T(8,128)(2,1)S(1)}, bf16[4,8,576]{2,1,0:T(8,128)(2,1)}, u32[]{:S(2)}, u32[]{:S(2)}) collective-permute-start(bf16[4,8,576]{2,1,0:T(8,128)(2,1)S(1)} %collective-permute-done.4), channel_id=1, source_target_pairs={{0,14},{2,0},{4,2},{6,4},{8,6},{10,8},{12,10},{14,12},{1,15},{3,1}... | collective-permute-start | bytes 110600 | tf_op jit(solution)/shard_map/ppermute | solution.py:34
  32.0 1.2 %collective-permute-done.2 = bf16[4,8,576]{2,1,0:T(8,128)(2,1)} collective-permute-done((bf16[4,8,576]{2,1,0:T(8,128)(2,1)S(1)}, bf16[4,8,576]{2,1,0:T(8,128)(2,1)}, u32[]{:S(2)}, u32[]{:S(2)}) %collective-permute-start.2) | collective-permute-done | bytes 36896 | tf_op jit(solution)/shard_map/ppermute | solution.py:32
  33.7 5.1 %collective-permute-start.6 = (bf16[4,8,576]{2,1,0:T(8,128)(2,1)}, bf16[4,8,576]{2,1,0:T(8,128)(2,1)S(1)}, u32[]{:S(2)}, u32[]{:S(2)}) collective-permute-start(bf16[4,8,576]{2,1,0:T(8,128)(2,1)} %collective-permute-done.5), channel_id=1, source_target_pairs={{0,14},{2,0},{4,2},{6,4},{8,6},{10,8},{12,10},{14,12},{1,15},{3,1}... | collective-permute-start | bytes 110600 | tf_op jit(solution)/shard_map/ppermute | solution.py:34
  38.8 1.4 %collective-permute-done.3 = bf16[4,8,576]{2,1,0:T(8,128)(2,1)} collective-permute-done((bf16[4,8,576]{2,1,0:T(8,128)(2,1)}, bf16[4,8,576]{2,1,0:T(8,128)(2,1)}, u32[]{:S(2)}, u32[]{:S(2)}) %collective-permute-start.3) | collective-permute-done | bytes 36896 | tf_op jit(solution)/shard_map/ppermute | solution.py:32
  41.1 0.8 constant_dynamic-update-slice_fusion.14
  41.8 0.8 constant_dynamic-update-slice_fusion.13
  42.7 0.8 constant_dynamic-update-slice_fusion.9
  43.5 0.8 constant_dynamic-update-slice_fusion.7
  45.1 0.8 constant_dynamic-update-slice_fusion.5
  45.9 0.8 constant_dynamic-update-slice_fusion.1
  46.7 0.8 copy-done.3
  47.6 1.3 %convolution_multiply_fusion = f32[4,64,512]{2,1,0:T(8,128)} fusion(bf16[4,512,576]{1,2,0:T(8,128)(2,1)S(1)} %copy-done.1, bf16[4,128,576]{2,1,0:T(8,128)(2,1)S(1)} %constant_dynamic-update-slice_fusion, s32[]{:T(128)S(6)} %select_n.79), kind=kOutput, calls=%fused_computation.6 | convolution fusion | flops 151126016 | bytes 3211268 | tf_op jit(solution)/shard_map/rhd,rtd->rht/dot_general | solution.py:74
  48.9 1.2 %reshape.136 = f32[4,64,8,64]{3,2,1,0:T(8,128)S(1)} reshape(f32[4,64,512]{2,1,0:T(8,128)} %convolution_multiply_fusion) | data formatting | bytes 1048576 | tf_op jit(solution)/shard_map/reshape | solution.py:77
  51.9 3.5 %all-to-all-start.2 = ((f32[4,8,8]{2,0,1:T(4,128)}), f32[4,8,8]{2,0,1:T(4,128)S(1)}, u32[]{:S(2)}, u32[]{:S(2)}) async-start(f32[4,8,8]{2,0,1:T(4,128)} %copy.104), calls=%async_computation.2 | async-start | bytes 32768 | tf_op jit(solution)/shard_map/all_to_all | solution.py:102
  55.5 4.3 %convolution_bitcast_fusion = f32[4,64,8,512]{3,1,2,0:T(8,128)} fusion(bf16[4,8,64,576]{3,2,1,0:T(8,128)(2,1)} %bitcast.21, f32[4,64,8,64]{3,2,1,0:T(8,128)S(1)} %reshape.136, f32[4,64,8]{1,2,0:T(8,128)S(1)} %fusion.5, pred[4,8,64]{2,1,0:T(8,128)(4,1)S(1)} %broadcast_compare_fusion), kind=kOutput, calls=%fused_computation.4 | convolution fusion | flops 134742016 | bytes 6825984 | tf_op jit(solution)/shard_map/rhpt,rptl->rhpl/dot_general | solution.py:84
  60.5 1.5 %all-to-all-done.2 = f32[4,8,8]{2,0,1:T(4,128)S(1)} async-done(((f32[4,8,8]{2,0,1:T(4,128)}), f32[4,8,8]{2,0,1:T(4,128)S(1)}, u32[]{:S(2)}, u32[]{:S(2)}) %all-to-all-start.2) | async-done | bytes 1056 | tf_op jit(solution)/shard_map/all_to_all | solution.py:102
  62.1 4.5 %all-to-all-start = ((f32[4,8,8]{2,0,1:T(4,128)}), f32[4,8,8]{2,0,1:T(4,128)S(1)}, u32[]{:S(2)}, u32[]{:S(2)}) async-start(f32[4,8,8]{2,0,1:T(4,128)} %copy.101), calls=%async_computation | async-start | bytes 32768 | tf_op jit(solution)/shard_map/all_to_all | solution.py:95
  66.6 8.2 %fusion = f32[4,64,1,512]{3,2,1,0:T(1,128)S(1)} fusion(f32[4,64,8,1]{2,3,1,0:T(1,128)S(1)} %copy.108, f32[4,64,8,512]{3,1,2,0:T(8,128)} %convolution_bitcast_fusion), kind=kOutput, calls=%fused_computation | convolution fusion | flops 12582912 | bytes 4726784 | tf_op jit(solution)/shard_map/rhp,rhpl->rhl/dot_general | solution.py:93
  74.9 0.8 copy.103
  75.7 6.0 %all-to-all-start.1 = ((f32[4,8,8,512]{3,2,0,1:T(8,128)}), f32[4,8,8,512]{3,2,0,1:T(8,128)S(1)}, u32[]{:S(2)}, u32[]{:S(2)}) async-start(f32[4,8,8,512]{3,2,0,1:T(8,128)} %copy.103), calls=%async_computation.1 | async-start | bytes 1048576 | tf_op jit(solution)/shard_map/all_to_all | solution.py:109
  83.1 3.4 %pmax.7 = f32[4,8,8]{2,1,0:T(8,128)S(1)} all-reduce(f32[4,8,8]{2,1,0:T(8,128)S(1)} %select_reduce_fusion.2), channel_id=1, replica_groups=mesh['grp'=2,'seq'=8,'head'=2] {'head'}, use_global_device_ids=true, to_apply=%region_12.13 | all-reduce | flops 256 | bytes 2048 | tf_op jit(solution)/shard_map/pmax | solution.py:69
  87.2 4.8 %all-to-all-done.1 = f32[4,8,8,512]{3,2,0,1:T(8,128)S(1)} async-done(((f32[4,8,8,512]{3,2,0,1:T(8,128)}), f32[4,8,8,512]{3,2,0,1:T(8,128)S(1)}, u32[]{:S(2)}, u32[]{:S(2)}) %all-to-all-start.1) | async-done | bytes 524320 | tf_op jit(solution)/shard_map/all_to_all | solution.py:109
  (66 shorter events, 9.7 us)
Async XLA Ops:
  0.6 1.2 %copy-start = (bf16[8,128,512]{2,1,0:T(8,128)(2,1)S(1)}, bf16[8,128,512]{2,1,0:T(8,128)(2,1)}, u32[]{:S(2)}) copy-start(bf16[8,128,512]{2,1,0:T(8,128)(2,1)} %param.9) | copy-start | bytes 3145732
  4.1 15.6 %collective-permute-start = (bf16[4,8,576]{2,1,0:T(8,128)(2,1)}, bf16[4,8,576]{2,1,0:T(8,128)(2,1)S(1)}, u32[]{:S(2)}, u32[]{:S(2)}) collective-permute-start(bf16[4,8,576]{2,1,0:T(8,128)(2,1)} %pad_maximum_fusion), channel_id=1, source_target_pairs={{0,2},{2,4},{4,6},{6,8},{8,10},{10,12},{12,14},{14,0},{1,3},{3,5},... | collective-permute-start | bytes 110600 | tf_op jit(solution)/shard_map/ppermute | solution.py:32
  7.1 20.1 %collective-permute-start.4 = (bf16[4,8,576]{2,1,0:T(8,128)(2,1)}, bf16[4,8,576]{2,1,0:T(8,128)(2,1)S(1)}, u32[]{:S(2)}, u32[]{:S(2)}) collective-permute-start(bf16[4,8,576]{2,1,0:T(8,128)(2,1)} %pad_maximum_fusion), channel_id=1, source_target_pairs={{0,14},{2,0},{4,2},{6,4},{8,6},{10,8},{12,10},{14,12},{1,15},{3,1}... | collective-permute-start | bytes 110600 | tf_op jit(solution)/shard_map/ppermute | solution.py:34
  11.4 8.4 %copy-start.9 = (s32[4,8,32]{2,1,0:T(8,128)S(1)}, s32[4,8,32]{2,1,0:T(8,128)}, u32[]{:S(2)}) copy-start(s32[4,8,32]{2,1,0:T(8,128)} %param.13) | copy-start | bytes 12292
  15.7 26.9 %copy-start.6 = (bf16[4,8,64]{2,1,0:T(8,128)(2,1)S(1)}, bf16[4,8,64]{2,1,0:T(8,128)(2,1)}, u32[]{:S(2)}) copy-start(bf16[4,8,64]{2,1,0:T(8,128)(2,1)} %param.8) | copy-start | bytes 12292
  15.7 31.8 %copy-start.1 = (bf16[4,512,576]{1,2,0:T(8,128)(2,1)S(1)}, bf16[4,512,576]{1,2,0:T(8,128)(2,1)}, u32[]{:S(2)}) copy-start(bf16[4,512,576]{1,2,0:T(8,128)(2,1)} %param.11) | copy-start | bytes 7077892
  19.8 6.7 %collective-permute-start.1 = (bf16[4,8,576]{2,1,0:T(8,128)(2,1)S(1)}, bf16[4,8,576]{2,1,0:T(8,128)(2,1)S(1)}, u32[]{:S(2)}, u32[]{:S(2)}) collective-permute-start(bf16[4,8,576]{2,1,0:T(8,128)(2,1)S(1)} %collective-permute-done), channel_id=1, source_target_pairs={{0,2},{2,4},{4,6},{6,8},{8,10},{10,12},{12,14},{14,0},{1,3},{3,5},... | collective-permute-start | bytes 110600 | tf_op jit(solution)/shard_map/ppermute | solution.py:32
  26.5 0.8 copy-start.5
  26.5 6.8 %collective-permute-start.2 = (bf16[4,8,576]{2,1,0:T(8,128)(2,1)S(1)}, bf16[4,8,576]{2,1,0:T(8,128)(2,1)}, u32[]{:S(2)}, u32[]{:S(2)}) collective-permute-start(bf16[4,8,576]{2,1,0:T(8,128)(2,1)S(1)} %collective-permute-done.1), channel_id=1, source_target_pairs={{0,2},{2,4},{4,6},{6,8},{8,10},{10,12},{12,14},{14,0},{1,3},{3,5},... | collective-permute-start | bytes 110600 | tf_op jit(solution)/shard_map/ppermute | solution.py:32
  27.3 6.4 %collective-permute-start.5 = (bf16[4,8,576]{2,1,0:T(8,128)(2,1)S(1)}, bf16[4,8,576]{2,1,0:T(8,128)(2,1)}, u32[]{:S(2)}, u32[]{:S(2)}) collective-permute-start(bf16[4,8,576]{2,1,0:T(8,128)(2,1)S(1)} %collective-permute-done.4), channel_id=1, source_target_pairs={{0,14},{2,0},{4,2},{6,4},{8,6},{10,8},{12,10},{14,12},{1,15},{3,1}... | collective-permute-start | bytes 110600 | tf_op jit(solution)/shard_map/ppermute | solution.py:34
  33.3 7.0 %collective-permute-start.3 = (bf16[4,8,576]{2,1,0:T(8,128)(2,1)}, bf16[4,8,576]{2,1,0:T(8,128)(2,1)}, u32[]{:S(2)}, u32[]{:S(2)}) collective-permute-start(bf16[4,8,576]{2,1,0:T(8,128)(2,1)} %collective-permute-done.2), channel_id=1, source_target_pairs={{0,2},{2,4},{4,6},{6,8},{8,10},{10,12},{12,14},{14,0},{1,3},{3,5},... | collective-permute-start | bytes 110600 | tf_op jit(solution)/shard_map/ppermute | solution.py:32
  33.7 9.8 %collective-permute-start.6 = (bf16[4,8,576]{2,1,0:T(8,128)(2,1)}, bf16[4,8,576]{2,1,0:T(8,128)(2,1)S(1)}, u32[]{:S(2)}, u32[]{:S(2)}) collective-permute-start(bf16[4,8,576]{2,1,0:T(8,128)(2,1)} %collective-permute-done.5), channel_id=1, source_target_pairs={{0,14},{2,0},{4,2},{6,4},{8,6},{10,8},{12,10},{14,12},{1,15},{3,1}... | collective-permute-start | bytes 110600 | tf_op jit(solution)/shard_map/ppermute | solution.py:34
  46.7 0.8 copy-start.3
  51.9 10.1 %all-to-all-start.2 = ((f32[4,8,8]{2,0,1:T(4,128)}), f32[4,8,8]{2,0,1:T(4,128)S(1)}, u32[]{:S(2)}, u32[]{:S(2)}) async-start(f32[4,8,8]{2,0,1:T(4,128)} %copy.104), calls=%async_computation.2 | async-start | bytes 32768 | tf_op jit(solution)/shard_map/all_to_all | solution.py:102
  62.1 13.6 %all-to-all-start = ((f32[4,8,8]{2,0,1:T(4,128)}), f32[4,8,8]{2,0,1:T(4,128)S(1)}, u32[]{:S(2)}, u32[]{:S(2)}) async-start(f32[4,8,8]{2,0,1:T(4,128)} %copy.101), calls=%async_computation | async-start | bytes 32768 | tf_op jit(solution)/shard_map/all_to_all | solution.py:95
  74.8 6.9 %copy-start.4 = (bf16[4,128,576]{2,1,0:T(8,128)(2,1)S(1)}, bf16[4,128,576]{2,1,0:T(8,128)(2,1)}, u32[]{:S(2)}) copy-start(bf16[4,128,576]{2,1,0:T(8,128)(2,1)} %copy-done.3) | copy-start | bytes 1769476
  74.8 6.9 %copy-start.7 = (bf16[4,8,576]{2,1,0:T(8,128)(2,1)S(1)}, bf16[4,8,576]{2,1,0:T(8,128)(2,1)}, u32[]{:S(2)}) copy-start(bf16[4,8,576]{2,1,0:T(8,128)(2,1)} %get-tuple-element.18) | copy-start | bytes 110596
  74.8 6.9 %copy-start.8 = (bf16[4,8,576]{2,1,0:T(8,128)(2,1)S(1)}, bf16[4,8,576]{2,1,0:T(8,128)(2,1)}, u32[]{:S(2)}) copy-start(bf16[4,8,576]{2,1,0:T(8,128)(2,1)} %get-tuple-element.19) | copy-start | bytes 110596
  74.8 8.2 %copy-start.10 = (pred[8,64]{1,0:T(8,128)(4,1)S(1)}, pred[8,64]{1,0:T(8,128)(4,1)}, u32[]{:S(2)}) copy-start(pred[8,64]{1,0:T(8,128)(4,1)} %iota_compare_fusion) | copy-start | bytes 1540
  74.8 17.4 %copy-start.2 = (bf16[8,512,128]{2,1,0:T(8,128)(2,1)S(1)}, bf16[8,512,128]{2,1,0:T(8,128)(2,1)}, u32[]{:S(2)}) copy-start(bf16[8,512,128]{2,1,0:T(8,128)(2,1)} %param.10) | copy-start | bytes 3145732
  75.7 16.3 %all-to-all-start.1 = ((f32[4,8,8,512]{3,2,0,1:T(8,128)}), f32[4,8,8,512]{3,2,0,1:T(8,128)S(1)}, u32[]{:S(2)}, u32[]{:S(2)}) async-start(f32[4,8,8,512]{3,2,0,1:T(8,128)} %copy.103), calls=%async_computation.1 | async-start | bytes 1048576 | tf_op jit(solution)/shard_map/all_to_all | solution.py:109
